TPU v7x, 256 devices: a whole 4x4x8 slice. The times are simulated.
256 devices in a mesh: ctx: 64 (over x, z, y_hi), tp: 4 (over y_lo, core).
Axes of the slice: x: 4, y: 4 (y_hi: 2, y_lo: 2; y = y_hi * 2 + y_lo), z: 8, core: 2. Of those that a mesh axis runs over, the one named last changes fastest.
Arguments:
- tokens: bfloat16 [16384, 8192], P('ctx'), may hold values from -6 to 6
- select_index: int32 [2048], P('ctx'), may hold values from 0 to 255, as said below
- valid_count: int32 [64], replicated, may hold values from 4 to 32, as said below
- queries: bfloat16 [2048, 4096], P('ctx', 'tp'), may hold values from -160 to 160
- key_matrix: bfloat16 [8192, 512], P('ctx', 'tp'), may hold values from -0.0625 to 0.0625
- value_matrix: bfloat16 [8192, 512], P('ctx', 'tp'), may hold values from -0.0625 to 0.0625
- out_grad: bfloat16 [2048, 4096], P('ctx', 'tp'), may hold values from -6 to 6
Outputs:
- attended: bfloat16 [2048, 4096], P('ctx', 'tp')
- query_gradient: bfloat16 [2048, 4096], P('ctx', 'tp')
- token_grad: bfloat16 [16384, 8192], P('ctx', 'tp')
- key_weight_grad: bfloat16 [8192, 512], P('ctx', 'tp')
- value_weight_grad: bfloat16 [8192, 512], P('ctx', 'tp')
Inputs may be any that keep to these rules, and one draw needn't show every extreme that they name: `select_index`: within one shard the offsets of all 32 slots are distinct, and those of the first valid_count slots rise. `valid_count`: some shard holds exactly 32 live slots.
All inputs are finite; a program needn't handle non-finite values.
Results may differ from a plain program's by a relative error of at most 0.023.
The roundings to bfloat16 on the way count: a program that leaves them out, or rounds other values in their place, can miss the bound.
Values may be sent and summed in bfloat16 or wider, within the bound.
A program may use at most 64 MiB of HBM per device.

v0:
```python
import math
import jax
import jax.numpy as jnp
from jax import lax
from jax.sharding import PartitionSpec as P

HEAD_WIDTH = 128
neg_large = -1e30


def local(tokens, select_index, valid_count, queries, key_matrix, value_matrix, out_grad):
    shard_len = tokens.shape[0]
    capacity = select_index.shape[0]
    key_value_width = key_matrix.shape[1]
    kv_local = key_value_width // HEAD_WIDTH
    per_group = queries.shape[1] // key_value_width
    ctx_size = lax.axis_size("ctx")
    own_shard = lax.axis_index("ctx")
    all_keys = ctx_size * capacity
    block_len = min(512, all_keys)
    num_blocks = all_keys // block_len
    score_scale = 1.0 / math.sqrt(HEAD_WIDTH)
    slot_ids = jnp.arange(capacity, dtype=jnp.int32)
    own_count = jnp.sum(
        jnp.where(jnp.arange(ctx_size, dtype=jnp.int32) == own_shard, valid_count, 0)
    )
    live_query = slot_ids < own_count
    query_pos = jnp.where(live_query, select_index, shard_len)
    key_shard = jnp.arange(all_keys, dtype=jnp.int32) // capacity
    key_live = (slot_ids[None, :] < valid_count[:, None]).reshape(all_keys)
    key_pos = jnp.tile(select_index, ctx_size)
    picked = jnp.take(tokens, select_index, axis=0)
    weight_key, weight_value = (
        lax.all_gather(key_matrix, "ctx", axis=0, tiled=True),
        lax.all_gather(value_matrix, "ctx", axis=0, tiled=True),
    )
    both_weights = jnp.concatenate([weight_key, weight_value], axis=1)
    projected = jnp.dot(picked, both_weights, preferred_element_type=jnp.float32).astype(
        jnp.bfloat16
    )
    kv_rows = lax.all_gather(projected, "ctx", axis=0, tiled=True)
    heads_of_query = queries.reshape(capacity, kv_local, per_group, HEAD_WIDTH)
    gradient_rows = jnp.where(live_query[:, None], out_grad, jnp.zeros_like(out_grad))
    gradient_heads = gradient_rows.reshape(capacity, kv_local, per_group, HEAD_WIDTH)
    stat_shape = (kv_local, per_group, capacity)

    def block_data(blk_id):
        leading_item = blk_id * block_len
        kv_blk = lax.dynamic_slice_in_dim(kv_rows, leading_item, block_len, 0)
        key_block = kv_blk[:, :key_value_width].reshape(block_len, kv_local, HEAD_WIDTH)
        value_block = kv_blk[:, key_value_width:].reshape(block_len, kv_local, HEAD_WIDTH)
        live_blk = lax.dynamic_slice_in_dim(key_live, leading_item, block_len, 0)
        shard_blk = lax.dynamic_slice_in_dim(key_shard, leading_item, block_len, 0)
        pos_blk = lax.dynamic_slice_in_dim(key_pos, leading_item, block_len, 0)
        same_shard = (shard_blk[None, :] == own_shard) & (pos_blk[None, :] <= query_pos[:, None])
        visible = live_blk[None, :] & ((shard_blk[None, :] < own_shard) | same_shard)
        active = leading_item // capacity <= own_shard
        return (key_block, value_block, visible, active)

    def block_scores(key_block, visible):
        scores = (
            jnp.einsum(
                "toul,iol->outi", heads_of_query, key_block, preferred_element_type=jnp.float32
            )
            * score_scale
        )
        return jnp.where(visible[None, None], scores, neg_large)

    def max_step(carried, blk_id):
        row_max, row_sum = carried
        key_block, value_block, visible, active = block_data(blk_id)

        def max_visit():
            scores = block_scores(key_block, visible)
            new_max = jnp.maximum(row_max, jnp.max(scores, axis=-1))
            terms = jnp.where(visible[None, None], jnp.exp(scores - new_max[..., None]), 0.0)
            new_sum = row_sum * jnp.exp(row_max - new_max) + jnp.sum(terms, axis=-1)
            return ((new_max, new_sum), scores)

        def max_ignore():
            return ((row_max, row_sum), jnp.full(stat_shape + (block_len,), neg_large, jnp.float32))

        stats, scores = lax.cond(active, max_visit, max_ignore)
        return (stats, None)

    start_stats = (jnp.full(stat_shape, neg_large, jnp.float32), jnp.zeros(stat_shape, jnp.float32))
    block_ids = jnp.arange(num_blocks, dtype=jnp.int32)
    (row_max, row_sum), stored = lax.scan(max_step, start_stats, block_ids)
    log_total = row_max + jnp.log(row_sum)

    def get_scores(key_block, visible):
        return block_scores(key_block, visible)

    def out_step(output_acc, blk_id):
        key_block, value_block, visible, active = block_data(blk_id)

        def out_visit():
            probs = jnp.exp(get_scores(key_block, visible) - log_total[..., None])
            weight_matrices = probs.astype(jnp.bfloat16)
            return output_acc + jnp.einsum(
                "ljvo,olf->vljf", weight_matrices, value_block, preferred_element_type=jnp.float32
            )

        def out_ignore():
            return output_acc

        return (lax.cond(active, out_visit, out_ignore), None)

    head_shape = (capacity, kv_local, per_group, HEAD_WIDTH)
    output_acc, unused = lax.scan(out_step, jnp.zeros(head_shape, jnp.float32), block_ids)
    attended = jnp.where(live_query[:, None, None, None], output_acc, 0.0).astype(jnp.bfloat16)
    out_dot = jnp.transpose(
        jnp.sum(gradient_heads.astype(jnp.float32) * attended.astype(jnp.float32), axis=-1),
        (1, 2, 0),
    )

    def grad_step(query_acc, blk_id):
        key_block, value_block, visible, active = block_data(blk_id)

        def grad_visit():
            probs = jnp.exp(get_scores(key_block, visible) - log_total[..., None])
            weight_matrices = probs.astype(jnp.bfloat16)
            grad_probs = jnp.einsum(
                "toul,iol->outi", gradient_heads, value_block, preferred_element_type=jnp.float32
            )
            score_gradient = (probs * (grad_probs - out_dot[..., None]) * score_scale).astype(
                jnp.bfloat16
            )
            new_acc = query_acc + jnp.einsum(
                "ljvo,olf->vljf", score_gradient, key_block, preferred_element_type=jnp.float32
            )
            key_part = jnp.einsum(
                "cifh,fcij->hcj", score_gradient, heads_of_query, preferred_element_type=jnp.float32
            )
            value_part = jnp.einsum(
                "cifh,fcij->hcj",
                weight_matrices,
                gradient_heads,
                preferred_element_type=jnp.float32,
            )
            return (
                new_acc,
                jnp.concatenate(
                    [
                        key_part.reshape(block_len, key_value_width),
                        value_part.reshape(block_len, key_value_width),
                    ],
                    axis=1,
                ),
            )

        def grad_ignore():
            return (query_acc, jnp.zeros((block_len, 2 * key_value_width), jnp.float32))

        return lax.cond(active, grad_visit, grad_ignore)

    query_acc, kv_terms = lax.scan(grad_step, jnp.zeros(head_shape, jnp.float32), block_ids)
    query_gradient = query_acc.astype(jnp.bfloat16).reshape(
        capacity, kv_local * per_group * HEAD_WIDTH
    )
    kv_terms = kv_terms.reshape(all_keys, 2 * key_value_width)
    own_grads = lax.psum_scatter(kv_terms, "ctx", scatter_dimension=0, tiled=True).astype(
        jnp.bfloat16
    )
    weight_grad = lax.psum_scatter(
        lax.dot_general(
            picked, own_grads, (((0,), (0,)), ((), ())), preferred_element_type=jnp.float32
        ),
        "ctx",
        scatter_dimension=0,
        tiled=True,
    )
    key_weight_grad = weight_grad[:, :key_value_width].astype(jnp.bfloat16)
    value_weight_grad = weight_grad[:, key_value_width:].astype(jnp.bfloat16)
    row_grad = lax.dot_general(
        own_grads, both_weights, (((1,), (1,)), ((), ())), preferred_element_type=jnp.float32
    )
    summed = lax.psum_scatter(row_grad, "tp", scatter_dimension=1, tiled=True)
    summed = jnp.where(live_query[:, None], summed, 0.0)
    token_grad = (
        jnp.zeros((shard_len, summed.shape[1]), jnp.float32)
        .at[select_index]
        .set(summed)
        .astype(jnp.bfloat16)
    )
    return (
        attended.reshape(capacity, kv_local * per_group * HEAD_WIDTH),
        query_gradient,
        token_grad,
        key_weight_grad,
        value_weight_grad,
    )


def solution(mesh):
    in_specs = (
        P("ctx", None),
        P("ctx"),
        P(),
        P("ctx", "tp"),
        P("ctx", "tp"),
        P("ctx", "tp"),
        P("ctx", "tp"),
    )
    out_specs = (P("ctx", "tp"), P("ctx", "tp"), P("ctx", "tp"), P("ctx", "tp"), P("ctx", "tp"))
    return jax.shard_map(local, mesh=mesh, in_specs=in_specs, out_specs=out_specs, check_vma=False)
```

profile of v0, /device:TPU:8, one launch (start us, length us, event | category | flops | bytes accessed | tf_op | source)
XLA Modules:
  0.0 1205.8 jit_solution(602995603653789307)
XLA Ops:
  7.2 0.7 all-gather.4.cloned.1.call-update
  7.9 0.7 all-gather.6.cloned.1.call-update
  8.7 1.3 fusion.76
  10.0 1.2 broadcast_select_fusion.3
  11.2 4.1 gather_fusion
  15.3 116.2 %all-gather.4.cloned.1.call-done = bf16[8192,128]{1,0:T(8,128)(2,1)} async-done(((bf16[128,128]{1,0:T(8,128)(2,1)}), bf16[8192,128]{1,0:T(8,128)(2,1)}) %all-gather.4.cloned.1.call-update) | async-done | bytes 2097168 | tf_op jit(solution)/shard_map/all_gather | solution.py:34
  131.5 3.2 constant_dynamic-update-slice_fusion.2
  134.7 114.9 %all-gather.6.cloned.1.call-done = bf16[8192,128]{1,0:T(8,128)(2,1)} async-done(((bf16[128,128]{1,0:T(8,128)(2,1)}), bf16[8192,128]{1,0:T(8,128)(2,1)}) %all-gather.6.cloned.1.call-update) | async-done | bytes 2097168 | tf_op jit(solution)/shard_map/all_gather | solution.py:35
  249.6 3.1 constant_dynamic-update-slice_fusion.1
  252.7 3.7 convolution_convert_fusion
  256.5 0.6 iota_compare_fusion
  257.2 110.9 %all-gather.8.cloned.1.call-done = bf16[2048,256]{1,0:T(8,128)(2,1)} async-done(((bf16[32,256]{1,0:T(8,128)(2,1)}), bf16[2048,256]{1,0:T(8,128)(2,1)}) %all-gather.8.cloned.1.call-update) | async-done | bytes 1048592 | tf_op jit(solution)/shard_map/all_gather | solution.py:41
  368.1 7.5 while.49
  368.2 0.6 dynamic_slice.201
  369.5 2.1 conditional.9
  369.5 0.1 broadcast_compare_fusion.2
  369.7 0.1 lt.166
  370.0 0.1 or_and_fusion
  370.1 1.2 fusion.80
  371.3 0.2 select_reduce_fusion
  371.6 0.6 dynamic_slice.201
  373.0 0.6 dynamic_slice.201
  374.3 0.6 dynamic_slice.201
  375.7 7.3 while.50
  375.7 0.6 dynamic_slice.202
  377.0 2.0 conditional.10
  377.0 0.1 broadcast_compare_fusion.5
  377.2 0.1 lt.169
  377.5 0.1 or_and_fusion.1
  377.6 1.4 fusion.31
  379.0 0.6 dynamic_slice.202
  380.3 0.6 dynamic_slice.202
  381.7 0.6 dynamic_slice.202
  383.0 0.2 multiply_reduce_fusion
  383.3 14.4 %while.51 = (s32[]{:T(128)}, f32[32,1,8,128]{3,0,2,1:T(8,128)S(1)}, f32[4,512,256]{2,1,0:T(8,128)}, s32[4]{0:T(128)S(1)}, s32[]{:T(128)}, /*index=5*/bf16[2048,2...) while((s32[]{:T(128)}, f32[32,1,8,128]{3,0,2,1:T(8,128)S(1)}, ...), condition=%wide.region_15.16_spmd.clone, body=%wide.region_12.15_spmd.clone.sunk | while | flops 169058832 | bytes 7068294 | solution.py:157
  383.3 0.6 dynamic_slice.203
  384.6 4.7 conditional.11
  385.1 0.1 or_and_fusion.2
  385.2 1.2 fusion.52
  386.4 1.2 fusion.53
  387.6 1.2 fusion.54
  388.8 0.2 convolution_bitcast_fusion.2
  389.0 0.2 convolution_bitcast_fusion.3
  389.3 0.2 copy.47
  389.5 0.8 constant_dynamic-update-slice_fusion.4
  390.4 0.6 dynamic_slice.203
  391.8 0.2 copy.47
  392.0 0.8 constant_dynamic-update-slice_fusion.4
  392.8 0.6 dynamic_slice.203
  394.2 0.2 copy.47
  394.4 0.9 constant_dynamic-update-slice_fusion.4
  395.3 0.6 dynamic_slice.203
  396.7 0.2 copy.47
  396.9 0.8 constant_dynamic-update-slice_fusion.4
  397.8 392.4 %reduce-scatter.4.cloned.1.call-done = f32[32,256]{1,0:T(8,128)} async-done(((f32[2048,256]{1,0:T(8,128)}), f32[32,256]{1,0:T(8,128)}) %reduce-scatter.4.cloned.1.call-update) | async-done | bytes 32784 | tf_op jit(solution)/shard_map/reduce_scatter | solution.py:162
  790.2 4.5 fusion.74
  794.8 4.6 fusion.69
  799.5 0.7 copy_bitcast_fusion
  800.2 9.3 reduce-scatter.6.cloned.1.call-done
  809.4 1.8 scatter_custom_fusion
  811.2 1.1 convert_element_type.73
  812.3 385.1 %reduce-scatter.8.cloned.1.call-done = f32[128,256]{1,0:T(8,128)} async-done(((f32[8192,256]{1,0:T(8,128)}), f32[128,256]{1,0:T(8,128)}) %reduce-scatter.8.cloned.1.call-update) | async-done | bytes 131088 | tf_op jit(solution)/shard_map/reduce_scatter | solution.py:165
  1197.4 0.9 convert.4
  1198.4 0.6 fusion.81
  (111 shorter events, 2.4 us)
Async XLA Ops:
  7.2 124.3 %all-gather.4.cloned.1.call-start = ((), (), s32[]{:S(2)}) async-start(), calls=%async_computation.3 | async-start | bytes 2129920 | tf_op jit(solution)/shard_map/all_gather | solution.py:34
  7.9 241.7 %all-gather.6.cloned.1.call-start = ((), (), s32[]{:S(2)}) async-start(), calls=%async_computation.4 | async-start | bytes 2129920 | tf_op jit(solution)/shard_map/all_gather | solution.py:35
  8.7 359.5 %all-gather.8.cloned.1.call-start = ((), (), s32[]{:S(2)}) async-start(), calls=%async_computation.5 | async-start | bytes 1064960 | tf_op jit(solution)/shard_map/all_gather | solution.py:41
  11.2 4.1 copy-start.1
  252.7 4.4 copy-start.3
  252.7 4.5 copy-start.4
  252.7 115.4 %copy-start.2 = (s32[64]{0:T(128)S(1)}, s32[64]{0:T(128)}, u32[]{:S(2)}) copy-start(s32[64]{0:T(128)} %param.21) | copy-start | bytes 772
  256.4 533.8 %reduce-scatter.4.cloned.1.call-start = ((), (), s32[]{:S(2)}) async-start(), calls=%async_computation.6 | async-start | bytes 2129920 | tf_op jit(solution)/shard_map/reduce_scatter | solution.py:162
  397.7 411.7 %reduce-scatter.6.cloned.1.call-start = ((), (), s32[]{:S(2)}) async-start(), calls=%async_computation.7 | async-start | bytes 1310720 | tf_op jit(solution)/shard_map/reduce_scatter | solution.py:178
  790.2 4.6 copy-start
  794.7 402.7 %reduce-scatter.8.cloned.1.call-start = ((), (), s32[]{:S(2)}) async-start(), calls=%async_computation.8 | async-start | bytes 8519680 | tf_op jit(solution)/shard_map/reduce_scatter | solution.py:165
Sparse Core Ops, SparseCore 0:
  11.6 119.8 all-gather.3
  135.1 114.4 all-gather.5
  256.5 111.5 all-gather.7
  397.9 392.2 reduce-scatter.3
  794.9 14.5 reduce-scatter.5
  811.8 385.5 reduce-scatter.7
where the time goes:
time: 1210 us
  waiting for transfers between devices  1130 us (93%)
  local copies, waits for them, and re-layouts  24.3 us (2%)
  matrix products  19.4 us (2%)
  between operations  14.3 us (1%)
    reduce_scatter x1, waiting for transfers between devices, local(): lax.psum_scatter(kv_terms, 'ctx', scatter_dimension=0, tiled=True)  392 us
    reduce_scatter x1, waiting for transfers between devices, local(): lax.psum_scatter(lax.dot_general(picked, own_grads, (((0,), (0,)), ((), (...  385 us
    all_gather x1, waiting for transfers between devices, local(): lax.all_gather(key_matrix, 'ctx', axis=0, tiled=True)  116 us
    all_gather x1, waiting for transfers between devices, local(): lax.all_gather(value_matrix, 'ctx', axis=0, tiled=True)  115 us
    all_gather x1, waiting for transfers between devices, local(): kv_rows = lax.all_gather(projected, 'ctx', axis=0, tiled=True)  111 us
  transfers between devices with their start and end apart: 6, of which 6 were waited for; matrix products, arithmetic and copies ran while one was open for 2% of the time, Pallas kernels for 0%

commit v1 on v0

--- a/solution.py
+++ b/solution.py
@@ -32,7 +32,9 @@
     picked = jnp.take(tokens, select_index, axis=0)
     weight_key, weight_value = (
         lax.all_gather(key_matrix, "ctx", axis=0, tiled=True),
-        lax.all_gather(value_matrix, "ctx", axis=0, tiled=True),
+        jnp.concatenate(
+            lax.all_to_all(jnp.stack([value_matrix] * lax.axis_size("ctx")), "ctx", 0, 0), axis=0
+        ),
     )
     both_weights = jnp.concatenate([weight_key, weight_value], axis=1)
     projected = jnp.dot(picked, both_weights, preferred_element_type=jnp.float32).astype(

time: 1210 us -> 1100 us (0.909)
  waiting for transfers between devices: 1130 us -> 1020 us
  starting transfers between devices: 0.24 us -> 14.3 us
    all_gather x1 -> x0, waiting for transfers between devices: 115 us -> none  [local(): lax.all_gather(value_matrix, 'ctx', axis=0, tiled=True)]
    all_to_all x0 -> x1, waiting for transfers between devices: none -> 47.3 us  [local(): lax.all_to_all(jnp.stack([value_matrix] * lax.axis_size('ctx')), 'ctx', 0...]
    all_gather x1, waiting for transfers between devices: 116 us -> 70.2 us  [local(): lax.all_gather(key_matrix, 'ctx', axis=0, tiled=True)]
    all_to_all x0 -> x1, starting transfers between devices: none -> 14.1 us  [local(): lax.all_to_all(jnp.stack([value_matrix] * lax.axis_size('ctx')), 'ctx', 0...]
  transfers between devices with their start and end apart: 6 -> 6, of which waited for: 6 -> 6; matrix products, arithmetic and copies ran while one was open for 2% -> 1% of each run, Pallas kernels for 0% -> 0%
where the time goes in v1:
time: 1100 us
  waiting for transfers between devices  1020 us (93%)
  local copies, waits for them, and re-layouts  20.6 us (2%)
  matrix products  19.5 us (2%)
  starting transfers between devices  14.3 us (1%)
  between operations  14 us (1%)
    reduce_scatter x1, waiting for transfers between devices, local(): lax.psum_scatter(kv_terms, 'ctx', scatter_dimension=0, tiled=True)  392 us
    reduce_scatter x1, waiting for transfers between devices, local(): lax.psum_scatter(lax.dot_general(picked, own_grads, (((0,), (0,)), ((), (...  385 us
    all_gather x1, waiting for transfers between devices, local(): kv_rows = lax.all_gather(projected, 'ctx', axis=0, tiled=True)  111 us
    all_gather x1, waiting for transfers between devices, local(): lax.all_gather(key_matrix, 'ctx', axis=0, tiled=True)  70.2 us
    all_to_all x1, waiting for transfers between devices, local(): lax.all_to_all(jnp.stack([value_matrix] * lax.axis_size('ctx')), 'ctx', 0...  47.3 us
  transfers between devices with their start and end apart: 6, of which 6 were waited for; matrix products, arithmetic and copies ran while one was open for 1% of the time, Pallas kernels for 0%

profile of v1, /device:TPU:8, one launch (start us, length us, event | category | flops | bytes accessed | tf_op | source)
XLA Modules:
  0.0 1100.1 jit_solution(16934943257048562452)
XLA Ops:
  7.2 2.6 stack.2
  9.8 14.1 %all-to-all-start = ((bf16[64,128,128]{2,1,0:T(8,128)(2,1)}), bf16[64,128,128]{2,1,0:T(8,128)(2,1)}, u32[]{:S(2)}, u32[]{:S(2)}) async-start(bf16[64,128,128]{2,1,0:T(8,128)(2,1)} %stack.2), calls=%async_computation | async-start | bytes 4194304 | tf_op jit(solution)/shard_map/all_to_all | solution.py:36
  23.9 0.7 all-gather.3.cloned.1.call-update
  24.7 0.7 fusion.78
  25.3 0.6 broadcast_select_fusion.3
  26.0 4.1 gather_fusion
  30.1 47.3 %all-to-all-done = bf16[64,128,128]{2,1,0:T(8,128)(2,1)} async-done(((bf16[64,128,128]{2,1,0:T(8,128)(2,1)}), bf16[64,128,128]{2,1,0:T(8,128)(2,1)}, u32[]{:S(2)}, u32[]{:S(2)}) %all-to-all-start) | async-done | bytes 2097184 | tf_op jit(solution)/shard_map/all_to_all | solution.py:36
  77.4 70.2 %all-gather.3.cloned.1.call-done = bf16[8192,128]{1,0:T(8,128)(2,1)} async-done(((bf16[128,128]{1,0:T(8,128)(2,1)}), bf16[8192,128]{1,0:T(8,128)(2,1)}) %all-gather.3.cloned.1.call-update) | async-done | bytes 2097168 | tf_op jit(solution)/shard_map/all_gather | solution.py:34
  147.7 3.7 fusion.68
  151.5 0.6 iota_compare_fusion
  152.3 111.1 %all-gather.5.cloned.1.call-done = bf16[2048,256]{1,0:T(8,128)(2,1)} async-done(((bf16[32,256]{1,0:T(8,128)(2,1)}), bf16[2048,256]{1,0:T(8,128)(2,1)}) %all-gather.5.cloned.1.call-update) | async-done | bytes 1048592 | tf_op jit(solution)/shard_map/all_gather | solution.py:43
  263.4 7.4 while.49
  263.4 0.6 dynamic_slice.201
  264.7 2.1 conditional.9
  264.9 0.1 broadcast_compare_fusion.2
  265.1 0.1 lt.166
  265.3 0.1 or_and_fusion
  265.4 1.2 fusion.84
  266.6 0.2 select_reduce_fusion
  266.9 0.6 dynamic_slice.201
  268.2 0.6 dynamic_slice.201
  269.6 0.6 dynamic_slice.201
  270.9 7.3 while.50
  271.0 0.6 dynamic_slice.202
  272.3 2.0 conditional.10
  272.4 0.1 broadcast_compare_fusion.5
  272.6 0.1 lt.169
  272.8 0.1 or_and_fusion.1
  272.9 1.4 fusion.31
  274.3 0.6 dynamic_slice.202
  275.6 0.6 dynamic_slice.202
  276.9 0.6 dynamic_slice.202
  278.3 0.2 multiply_reduce_fusion
  278.6 14.4 %while.51 = (s32[]{:T(128)}, f32[32,1,8,128]{3,0,2,1:T(8,128)S(1)}, f32[4,512,256]{2,1,0:T(8,128)}, s32[4]{0:T(128)S(1)}, s32[]{:T(128)}, /*index=5*/bf16[2048,2...) while((s32[]{:T(128)}, f32[32,1,8,128]{3,0,2,1:T(8,128)S(1)}, ...), condition=%wide.region_15.16_spmd.clone, body=%wide.region_12.15_spmd.clone.sunk | while | flops 169058832 | bytes 7068294 | solution.py:159
  278.6 0.6 dynamic_slice.203
  279.9 4.7 conditional.11
  280.2 0.1 lt.172
  280.4 0.1 or_and_fusion.2
  280.5 1.2 fusion.52
  281.7 1.2 fusion.53
  282.9 1.2 fusion.54
  284.1 0.2 convolution_bitcast_fusion.2
  284.3 0.2 convolution_bitcast_fusion.3
  284.6 0.2 copy.47
  284.8 0.8 constant_dynamic-update-slice_fusion.2
  285.6 0.6 dynamic_slice.203
  287.0 0.2 copy.47
  287.2 0.9 constant_dynamic-update-slice_fusion.2
  288.1 0.6 dynamic_slice.203
  289.5 0.2 copy.47
  289.7 0.9 constant_dynamic-update-slice_fusion.2
  290.5 0.6 dynamic_slice.203
  291.9 0.2 copy.47
  292.1 0.9 constant_dynamic-update-slice_fusion.2
  293.0 392.3 %reduce-scatter.4.cloned.1.call-done = f32[32,256]{1,0:T(8,128)} async-done(((f32[2048,256]{1,0:T(8,128)}), f32[32,256]{1,0:T(8,128)}) %reduce-scatter.4.cloned.1.call-update) | async-done | bytes 32784 | tf_op jit(solution)/shard_map/reduce_scatter | solution.py:164
  685.3 4.5 fusion.66
  690.0 4.6 fusion.72
  694.7 0.7 copy_bitcast_fusion
  695.3 9.1 reduce-scatter.6.cloned.1.call-done
  704.5 1.8 scatter_custom_fusion
  706.2 1.1 convert_element_type.73
  707.4 384.6 %reduce-scatter.8.cloned.1.call-done = f32[128,256]{1,0:T(8,128)} async-done(((f32[8192,256]{1,0:T(8,128)}), f32[128,256]{1,0:T(8,128)}) %reduce-scatter.8.cloned.1.call-update) | async-done | bytes 131088 | tf_op jit(solution)/shard_map/reduce_scatter | solution.py:167
  1092.0 0.9 convert.4
  1092.9 0.6 fusion.85
  (109 shorter events, 2.3 us)
Async XLA Ops:
  9.8 14.9 %copy-start.1 = (s32[64]{0:T(128)S(1)}, s32[64]{0:T(128)}, u32[]{:S(2)}) copy-start(s32[64]{0:T(128)} %param.21) | copy-start | bytes 772
  9.8 15.5 %copy-start = (s32[32]{0:T(128)S(1)}, s32[32]{0:T(128)}, u32[]{:S(2)}) copy-start(s32[32]{0:T(128)} %param.20) | copy-start | bytes 388
  9.8 67.6 %all-to-all-start = ((bf16[64,128,128]{2,1,0:T(8,128)(2,1)}), bf16[64,128,128]{2,1,0:T(8,128)(2,1)}, u32[]{:S(2)}, u32[]{:S(2)}) async-start(bf16[64,128,128]{2,1,0:T(8,128)(2,1)} %stack.2), calls=%async_computation | async-start | bytes 4194304 | tf_op jit(solution)/shard_map/all_to_all | solution.py:36
  23.9 123.8 %all-gather.3.cloned.1.call-start = ((), (), s32[]{:S(2)}) async-start(), calls=%async_computation.4 | async-start | bytes 2129920 | tf_op jit(solution)/shard_map/all_gather | solution.py:34
  24.6 238.8 %all-gather.5.cloned.1.call-start = ((), (), s32[]{:S(2)}) async-start(), calls=%async_computation.5 | async-start | bytes 1064960 | tf_op jit(solution)/shard_map/all_gather | solution.py:43
  147.7 3.8 copy-start.2
  147.7 4.5 copy-start.3
  151.4 533.9 %reduce-scatter.4.cloned.1.call-start = ((), (), s32[]{:S(2)}) async-start(), calls=%async_computation.6 | async-start | bytes 2129920 | tf_op jit(solution)/shard_map/reduce_scatter | solution.py:164
  293.0 411.5 %reduce-scatter.6.cloned.1.call-start = ((), (), s32[]{:S(2)}) async-start(), calls=%async_computation.7 | async-start | bytes 1310720 | tf_op jit(solution)/shard_map/reduce_scatter | solution.py:180
  685.3 4.6 copy-start.4
  689.9 402.1 %reduce-scatter.8.cloned.1.call-start = ((), (), s32[]{:S(2)}) async-start(), calls=%async_computation.8 | async-start | bytes 8519680 | tf_op jit(solution)/shard_map/reduce_scatter | solution.py:167
Sparse Core Ops, SparseCore 0:
  28.3 119.3 all-gather.2
  151.9 111.5 all-gather.4
  293.1 392.1 reduce-scatter.3
  690.0 14.3 reduce-scatter.5
  706.9 385.0 reduce-scatter.7
